TPU v7x, 256 devices: a whole 4x4x8 slice. The times are simulated.
256 devices in a mesh: ga: 16 (over z_lo, y), pair: 16 (over z_hi, x, core).
Axes of the slice: x: 4, y: 4, z: 8 (z_hi: 2, z_lo: 4; z = z_hi * 4 + z_lo), core: 2. Of those that a mesh axis runs over, the one named last changes fastest.
Arguments:
- val_density: bfloat16 [256, 3, 2, 8192], P('pair', None, None, 'ga'), may hold values from -0.0625 to 0.0625
- con_density: bfloat16 [576, 3, 2, 8192], P('ga', None, None, 'pair'), may hold values from -6 to 6
- screened: bfloat16 [3, 2, 8192, 8192], P(None, None, 'ga', 'pair'), may hold values from -0.0625 to 0.0625
- coulomb: float32 [3, 8192], P(None, 'ga'), may hold values from 0.2 to 2
- trans_here: bfloat16 [384, 2, 8192], P('pair', None, 'ga'), may hold values from -6 to 6
- trans_there: bfloat16 [384, 3, 2, 8192], P('pair', None, None, 'ga'), may hold values from -0.0625 to 0.0625
- shift_map: int32 [3, 8192], P(None, 'pair'), may hold values from 0 to 8191, as said below
- ordering: int32 [384], replicated, may hold values from 0 to 383, each once
Outputs:
- kernel: float32 [3, 2, 384, 384], P(None, None, 'pair', 'ga')
Inputs may be any that keep to these rules, and one draw needn't show every extreme that they name: `shift_map`: each aligned block of 128 entries of a row is a permutation of that block's own G-vector indices.
All inputs are finite; a program needn't handle non-finite values.
Results may differ from a plain program's by a relative error of at most 0.0003.
Values may be sent and summed in bfloat16 or wider, within the bound.
A program may use at most 64 MiB of HBM per device.

v0:
```python
import jax
import jax.numpy as jnp
from jax import lax
from jax.sharding import PartitionSpec as P

NV = 16
NC = 24
GBLK = 128
NT = 384


def contract_float(left, right):
    high = lax.Precision.HIGHEST
    real_part = jnp.einsum(
        "nkg,mkg->nkm", left[:, :, 0], right[:, :, 0], precision=high
    ) - jnp.einsum("nkg,mkg->nkm", left[:, :, 1], right[:, :, 1], precision=high)
    imag_part = jnp.einsum(
        "nkg,mkg->nkm", left[:, :, 0], right[:, :, 1], precision=high
    ) + jnp.einsum("nkg,mkg->nkm", left[:, :, 1], right[:, :, 0], precision=high)
    return jnp.stack([real_part, imag_part], axis=2)


def times_cols(rows, weights):
    first = jnp.einsum(
        "nkh,kgh->nkg", rows[:, :, 0], weights[:, 0], preferred_element_type=jnp.float32
    ) - jnp.einsum("nkh,kgh->nkg", rows[:, :, 1], weights[:, 1], preferred_element_type=jnp.float32)
    second = jnp.einsum(
        "nkh,kgh->nkg", rows[:, :, 0], weights[:, 1], preferred_element_type=jnp.float32
    ) + jnp.einsum("nkh,kgh->nkg", rows[:, :, 1], weights[:, 0], preferred_element_type=jnp.float32)
    return jnp.stack([first, second], axis=2)


def on_device(
    val_density, con_density, screened, coulomb, trans_here, trans_there, shift_map, ordering
):
    con_count = con_density.shape[0]
    points = con_density.shape[1]
    slab_cols = con_density.shape[3]
    blocks = slab_cols // GBLK
    within = (shift_map % GBLK).reshape(points, blocks, GBLK)
    onehot = (
        within[:, :, :, None] == jnp.arange(GBLK, dtype=jnp.int32)[None, None, None, :]
    ).astype(jnp.bfloat16)
    con_blocks = con_density.reshape(con_count, points, 2, blocks, GBLK)
    shifted = (
        jnp.einsum("bkpnh,kngh->bkpng", con_blocks, onehot, preferred_element_type=jnp.float32)
        .astype(jnp.bfloat16)
        .reshape(con_density.shape)
    )
    whole_here = lax.all_gather(trans_here, "pair", axis=0, tiled=True).astype(jnp.float32)
    weighted = trans_there.astype(jnp.float32) * coulomb[None, :, None, :]
    high = lax.Precision.HIGHEST
    exch_real = jnp.einsum(
        "tg,skg->tks", whole_here[:, 0], weighted[:, :, 0], precision=high
    ) - jnp.einsum("tg,skg->tks", whole_here[:, 1], weighted[:, :, 1], precision=high)
    exch_imag = jnp.einsum(
        "tg,skg->tks", whole_here[:, 0], weighted[:, :, 1], precision=high
    ) + jnp.einsum("tg,skg->tks", whole_here[:, 1], weighted[:, :, 0], precision=high)
    exch_part = jnp.stack([exch_real, exch_imag], axis=2)
    whole_con = lax.all_gather(shifted, "ga", axis=0, tiled=True)
    screened_rows = lax.psum_scatter(
        times_cols(whole_con, screened), "pair", scatter_dimension=0, tiled=True
    )
    direct_part = contract_float(
        lax.all_gather(val_density, "pair", axis=0, tiled=True).astype(jnp.float32), screened_rows
    )
    direct_sum, exch_sum = lax.psum((direct_part, exch_part), "ga")
    direct_full, exch_full = (
        lax.all_gather(direct_sum, "pair", axis=3, tiled=True),
        lax.all_gather(exch_sum, "pair", axis=3, tiled=True),
    )
    row_count = NT // lax.axis_size("pair")
    col_count = NT // lax.axis_size("ga")
    row_trans = lax.dynamic_slice_in_dim(ordering, lax.axis_index("pair") * row_count, row_count, 0)
    col_trans = lax.dynamic_slice_in_dim(ordering, lax.axis_index("ga") * col_count, col_count, 0)
    row_pairs = (row_trans // NC)[:, None] * NV + (col_trans // NC)[None, :]
    col_pairs = (row_trans % NC)[:, None] * NC + (col_trans % NC)[None, :]
    picked = direct_full[row_pairs.reshape(-1)]
    col_mask = (
        col_pairs.reshape(-1)[:, None] == jnp.arange(direct_full.shape[3], dtype=jnp.int32)[None, :]
    ).astype(jnp.float32)
    direct_flat = jnp.sum(picked * col_mask[:, None, None, :], axis=3)
    direct_sel = jnp.transpose(direct_flat.reshape(row_count, col_count, points, 2), (2, 3, 0, 1))
    exch_picked = exch_full[row_trans]
    col_hot = (jnp.arange(NT, dtype=jnp.int32)[:, None] == col_trans[None, :]).astype(jnp.float32)
    exch_sel = jnp.einsum("rkpt,tc->kprc", exch_picked, col_hot, precision=high)
    return 2.0 * exch_sel - direct_sel


def solution(mesh):
    in_specs = (
        P("pair", None, None, "ga"),
        P("ga", None, None, "pair"),
        P(None, None, "ga", "pair"),
        P(None, "ga"),
        P("pair", None, "ga"),
        P("pair", None, None, "ga"),
        P(None, "pair"),
        P(),
    )
    out_specs = P(None, None, "pair", "ga")
    return jax.shard_map(
        on_device, mesh=mesh, in_specs=in_specs, out_specs=out_specs, check_vma=False
    )
```

profile of v0, /device:TPU:1, one launch (start us, length us, event | category | flops | bytes accessed | tf_op | source)
XLA Modules:
  0.0 732.0 jit_solution(17700112051085489857)
XLA Ops:
  6.5 1.1 reshape.80
  7.6 0.7 add_select_fusion
  8.3 0.5 fusion.11
  8.8 0.1 copy.35
  8.9 0.8 reshape.81
  9.8 80.6 %all-gather.7.cloned.1.call-done = bf16[576,3,2,512]{3,2,1,0:T(2,128)(2,1)} async-done(((bf16[36,3,2,512]{3,2,1,0:T(2,128)(2,1)}), bf16[576,3,2,512]{3,2,1,0:T(2,128)(2,1)}) %all-gather.7.cloned.1.call-update) | async-done | bytes 3538960 | tf_op jit(solution)/shard_map/all_gather | solution.py:60
  90.4 9.1 %fusion.34 = (bf16[576,3,1,512]{3,2,1,0:T(2,128)(2,1)S(1)}, bf16[576,3,1,512]{3,2,1,0:T(2,128)(2,1)S(1)}) fusion(bf16[576,3,2,512]{3,2,1,0:T(2,128)(2,1)} %all-gather.7.cloned.1.call-done), kind=kLoop, calls=%fused_computation.75 | loop fusion | bytes 7077888 | tf_op jit(solution)/shard_map/slice | solution.py:26
  99.5 1.1 fusion.4
  100.6 1.1 fusion
  101.8 1.2 subtract_bitcast_fusion
  102.9 1.2 add_bitcast_fusion
  104.1 3.8 pad_maximum_fusion
  107.9 11.3 %copy.40 = f32[576,3,2,512]{3,2,1,0:T(2,128)} copy(f32[576,3,2,512]{3,0,1,2:T(8,128)} %pad_maximum_fusion) | data formatting | bytes 14155776 | tf_op jit(solution)/shard_map/stack | solution.py:30
  119.3 0.8 copy-done.3
  120.1 0.6 copy.42
  120.9 0.6 dynamic-slice
  122.2 47.9 %all_gather.15 = bf16[384,2,512]{2,0,1:T(8,128)(2,1)S(1)} all-gather(bf16[24,2,512]{2,0,1:T(8,128)(2,1)S(1)} %copy.31), channel_id=1, replica_groups=mesh['ga'=16,'pair'=16] {'pair'}, dimensions={0}, use_global_device_ids=true | all-gather | bytes 835584 | tf_op jit(solution)/shard_map/all_gather | solution.py:50
  170.1 0.5 fusion.24
  170.6 0.5 fusion.15
  171.1 0.5 fusion.23
  171.6 0.5 fusion.14
  172.1 0.7 pad_maximum_fusion.2
  172.8 168.5 %all-reduce.5.cloned.1.call-done = f32[576,3,2,512]{3,2,1,0:T(2,128)} async-done(((f32[576,3,2,512]{3,2,1,0:T(2,128)}), f32[576,3,2,512]{3,2,1,0:T(2,128)}) %all-reduce.5.cloned.1.call-update) | async-done | bytes 7077904
  341.3 1.5 constant_dynamic-slice_fusion
  342.8 64.9 %all-gather.9.cloned.1.call-done = bf16[256,3,2,512]{3,0,1,2:T(8,128)(2,1)} async-done(((bf16[16,3,2,512]{3,0,1,2:T(8,128)(2,1)}), bf16[256,3,2,512]{3,0,1,2:T(8,128)(2,1)}) %all-gather.9.cloned.1.call-update) | async-done | bytes 1572880 | tf_op jit(solution)/shard_map/all_gather | solution.py:65
  407.7 2.0 fusion.21
  409.7 1.9 fusion.20
  411.7 1.9 fusion.13
  413.6 0.8 fusion.12
  414.4 0.7 pad_maximum_fusion.1
  415.2 146.2 %all-reduce.7.cloned.1.call-done = (f32[384,3,2,24]{0,3,1,2:T(8,128)}, f32[256,3,2,36]{0,3,1,2:T(8,128)}) async-done(((f32[384,3,2,24]{0,3,1,2:T(8,128)}, f32[256,3,2,36]{0,3,1,2:T(8,128)}), (f32[384,3,2,24]{0,3,1,2:T(8,128)}, f32[256,3,2,36]{0,3,1,2:T(8,128)})) %all-reduce.7.cloned.1.call-update) | async-done | bytes 442384 | tf_op jit(solution)/shard_map/psum | solution.py:67
  561.3 1.8 copy.44
  563.2 0.5 all-gather.5.cloned.1.call-update
  563.7 0.1 fusion.32
  563.8 0.1 broadcast_add_fusion
  563.9 0.1 add.121
  564.0 0.1 add.129
  564.1 0.2 fusion.6
  564.3 80.0 %all-gather.11.cloned.1.call-done = f32[256,3,2,576]{0,2,1,3:T(2,128)} async-done(((f32[256,3,2,36]{0,2,1,3:T(2,128)}), f32[256,3,2,576]{0,2,1,3:T(2,128)}) %all-gather.11.cloned.1.call-update) | async-done | bytes 3538960 | tf_op jit(solution)/shard_map/all_gather | solution.py:69
  644.3 8.0 %copy.45 = f32[256,3,2,576]{3,2,1,0:T(2,128)} copy(f32[256,3,2,576]{0,2,1,3:T(2,128)} %all-gather.11.cloned.1.call-done) | data formatting | bytes 7077888 | tf_op jit(solution)/shard_map/all_gather | solution.py:69
  652.4 25.7 %gather_fusion.1 = f32[576,3,2,576]{3,2,1,0:T(2,128)} fusion(f32[256,3,2,576]{3,2,1,0:T(2,128)} %copy.45, s32[1024]{0:T(1024)S(1)} %pad_clamp_fusion), kind=kCustom, calls=%fused_computation.1 | custom fusion | bytes 15927552 | tf_op jit(solution)/shard_map/gather | solution.py:78
  678.1 6.7 multiply_reduce_fusion
  684.8 1.2 copy.47
  686.0 29.2 %all-gather.5.cloned.1.call-done = f32[384,3,2,384]{0,3,1,2:T(8,128)} async-done(((f32[384,3,2,24]{0,3,1,2:T(8,128)}), f32[384,3,2,384]{0,3,1,2:T(8,128)}) %all-gather.5.cloned.1.call-update) | async-done | bytes 3538960 | tf_op jit(solution)/shard_map/all_gather | solution.py:70
  715.3 6.2 copy.32
  721.5 1.5 gather_fusion
  722.9 1.5 fusion.17
  724.5 0.7 copy.48
  (33 shorter events, 0.4 us)
Async XLA Ops:
  6.5 83.9 %all-gather.7.cloned.1.call-start = ((), (), s32[]{:S(2)}) async-start(), calls=%async_computation.1 | async-start | bytes 3760128 | tf_op jit(solution)/shard_map/all_gather | solution.py:60
  9.7 89.8 %copy-start = (bf16[3,2,512,512]{3,2,1,0:T(8,128)(2,1)S(1)}, bf16[3,2,512,512]{3,2,1,0:T(8,128)(2,1)}, u32[]{:S(2)}) copy-start(bf16[3,2,512,512]{3,2,1,0:T(8,128)(2,1)} %param.10) | copy-start | bytes 9437188
  9.7 331.5 %all-reduce.5.cloned.1.call-start = ((), (), s32[]{:S(2)}) async-start(), calls=%async_computation.4 | async-start | bytes 14155776
  119.2 0.9 copy-start.3
  119.2 1.6 copy-start.4
  119.2 1.7 copy-start.7
  119.2 2.9 copy-start.2
  119.2 2.9 copy-start.5
  119.3 288.4 %all-gather.9.cloned.1.call-start = ((), (), s32[]{:S(2)}) async-start(), calls=%async_computation.2 | async-start | bytes 1671168 | tf_op jit(solution)/shard_map/all_gather | solution.py:65
  120.8 440.5 %all-reduce.7.cloned.1.call-start = ((), (), s32[]{:S(2)}) async-start(), calls=%async_computation.5 | async-start | bytes 933888 | tf_op jit(solution)/shard_map/psum | solution.py:67
  342.8 220.9 %copy-start.6 = (s32[384]{0:T(512)S(1)}, s32[384]{0:T(512)}, u32[]{:S(2)}) copy-start(s32[384]{0:T(512)} %param.15) | copy-start | bytes 4612
  407.7 5.9 copy-start.1
  415.1 229.2 %all-gather.11.cloned.1.call-start = ((), (), s32[]{:S(2)}) async-start(), calls=%async_computation.3 | async-start | bytes 3760128 | tf_op jit(solution)/shard_map/all_gather | solution.py:69
  563.1 152.2 %all-gather.5.cloned.1.call-start = ((), (), s32[]{:S(2)}) async-start(), calls=%async_computation | async-start | bytes 3760128 | tf_op jit(solution)/shard_map/all_gather | solution.py:70
Sparse Core Ops, SparseCore 0:
  9.8 80.5 all-gather.6
  119.4 221.8 all-reduce.4
  344.1 63.5 all-gather.8
  415.2 146.0 all-reduce.6
  563.9 80.4 all-gather.10
  646.9 68.3 all-gather.4
where the time goes:
time: 733 us; the launch traced here: 732 us
  waiting for transfers between devices  570 us (78%)
  local copies, waits for them, and re-layouts  71.3 us (10%)
  blocking collectives  47.9 us (7%)
  matrix products  15.1 us (2%)
  between operations  14.4 us (2%)
  other arithmetic  13 us (2%)
    unnamed x7, waiting for transfers between devices  169 us
    psum x1, waiting for transfers between devices, on_device(): direct_sum, exch_sum = lax.psum((direct_part, exch_part), 'ga')  146 us
    all_gather x1, waiting for transfers between devices, on_device(): whole_con = lax.all_gather(shifted, 'ga', axis=0, tiled=True)  80.6 us
    all_gather x1, waiting for transfers between devices, on_device(): lax.all_gather(direct_sum, 'pair', axis=3, tiled=True)  80 us
    all_gather x1, waiting for transfers between devices, on_device(): lax.all_gather(val_density, 'pair', axis=0, tiled=True).astype(jnp.float32)  64.9 us
    all_gather x1, blocking collectives, on_device(): lax.all_gather(trans_here, 'pair', axis=0, tiled=True).astype(jnp.float32)  47.9 us
    all_gather x1, waiting for transfers between devices, on_device(): lax.all_gather(exch_sum, 'pair', axis=3, tiled=True)  29.2 us
    gather x1, local copies, waits for them, and re-layouts, on_device(): picked = direct_full[row_pairs.reshape(-1)]  25.7 us
  transfers between devices with their start and end apart: 6, of which 6 were waited for; matrix products, arithmetic and copies ran while one was open for 7% of the time, Pallas kernels for 0%

commit v1 on v0

--- a/solution.py
+++ b/solution.py
@@ -7,6 +7,13 @@
 NC = 24
 GBLK = 128
 NT = 384
+
+
+def group_quarters(sample):
+    z_new = jnp.concatenate(
+        jax.lax.all_to_all(jnp.stack(jax.lax.psum(1, "pair") * [sample], axis=0), "pair", 0, 0), 3
+    )
+    return z_new
 
 
 def contract_float(left, right):
@@ -66,7 +73,7 @@
     )
     direct_sum, exch_sum = lax.psum((direct_part, exch_part), "ga")
     direct_full, exch_full = (
-        lax.all_gather(direct_sum, "pair", axis=3, tiled=True),
+        group_quarters(direct_sum),
         lax.all_gather(exch_sum, "pair", axis=3, tiled=True),
     )
     row_count = NT // lax.axis_size("pair")

time: 733 us -> 759 us (1.035); the launches traced: 732 us -> 749 us
  starting transfers between devices: 0.21 us -> 19 us
  waiting for transfers between devices: 570 us -> 556 us
  local copies, waits for them, and re-layouts: 71.3 us -> 79.1 us
    all_to_all x0 -> x1, waiting for transfers between devices: none -> 93.6 us  [group_quarters(): jax.lax.all_to_all(jnp.stack(jax.lax.psum(1, 'pair') * [sample], axis=0),...]
    all_gather x1 -> x0, waiting for transfers between devices: 80 us -> none  [on_device(): lax.all_gather(direct_sum, 'pair', axis=3, tiled=True)]
    all_gather x1, waiting for transfers between devices: 29.2 us -> 0.01 us  [on_device(): lax.all_gather(exch_sum, 'pair', axis=3, tiled=True)]
    all_to_all x0 -> x1, starting transfers between devices: none -> 18.8 us  [group_quarters(): jax.lax.all_to_all(jnp.stack(jax.lax.psum(1, 'pair') * [sample], axis=0),...]
    reshape x0 -> x2, local copies, waits for them, and re-layouts: none -> 11.3 us  [group_quarters(): jnp.concatenate(jax.lax.all_to_all(jnp.stack(jax.lax.psum(1, 'pair') * [s...]
    all_gather x1 -> x0, local copies, waits for them, and re-layouts: 8.04 us -> none  [on_device(): lax.all_gather(direct_sum, 'pair', axis=3, tiled=True)]
    unnamed x7 -> x6, waiting for transfers between devices: 169 us -> 171 us
  transfers between devices with their start and end apart: 6 -> 6, of which waited for: 6 -> 5; matrix products, arithmetic and copies ran while one was open for 7% -> 8% of each run, Pallas kernels for 0% -> 0%
where the time goes in v1:
time: 759 us; the launch traced here: 749 us
  waiting for transfers between devices  556 us (73%)
  local copies, waits for them, and re-layouts  79.1 us (10%)
  blocking collectives  47.9 us (6%)
  starting transfers between devices  19 us (3%)
  other arithmetic  17.2 us (2%)
  matrix products  15.1 us (2%)
  between operations  14.1 us (2%)
    unnamed x6, waiting for transfers between devices  171 us
    psum x1, waiting for transfers between devices, on_device(): direct_sum, exch_sum = lax.psum((direct_part, exch_part), 'ga')  146 us
    all_to_all x1, waiting for transfers between devices, group_quarters(): jax.lax.all_to_all(jnp.stack(jax.lax.psum(1, 'pair') * [sample], axis=0),...  93.6 us
    all_gather x1, waiting for transfers between devices, on_device(): whole_con = lax.all_gather(shifted, 'ga', axis=0, tiled=True)  80.6 us
    all_gather x1, waiting for transfers between devices, on_device(): lax.all_gather(val_density, 'pair', axis=0, tiled=True).astype(jnp.float32)  64.8 us
    all_gather x1, blocking collectives, on_device(): lax.all_gather(trans_here, 'pair', axis=0, tiled=True).astype(jnp.float32)  47.9 us
    gather x1, local copies, waits for them, and re-layouts, on_device(): picked = direct_full[row_pairs.reshape(-1)]  26.6 us
    all_to_all x1, starting transfers between devices, group_quarters(): jax.lax.all_to_all(jnp.stack(jax.lax.psum(1, 'pair') * [sample], axis=0),...  18.8 us
  transfers between devices with their start and end apart: 6, of which 5 were waited for; matrix products, arithmetic and copies ran while one was open for 8% of the time, Pallas kernels for 0%

profile of v1, /device:TPU:1, one launch (start us, length us, event | category | flops | bytes accessed | tf_op | source)
XLA Modules:
  0.0 748.5 jit_solution(1961435452112081598)
XLA Ops:
  6.5 0.7 add_select_fusion
  7.3 1.1 reshape.88
  8.9 0.8 reshape.89
  9.8 80.6 %all-gather.6.cloned.1.call-done = bf16[576,3,2,512]{3,2,1,0:T(2,128)(2,1)} async-done(((bf16[36,3,2,512]{3,2,1,0:T(2,128)(2,1)}), bf16[576,3,2,512]{3,2,1,0:T(2,128)(2,1)}) %all-gather.6.cloned.1.call-update) | async-done | bytes 3538960 | tf_op jit(solution)/shard_map/all_gather | solution.py:67
  90.4 9.1 %fusion.34 = (bf16[576,3,1,512]{3,2,1,0:T(2,128)(2,1)S(1)}, bf16[576,3,1,512]{3,2,1,0:T(2,128)(2,1)S(1)}) fusion(bf16[576,3,2,512]{3,2,1,0:T(2,128)(2,1)} %all-gather.6.cloned.1.call-done), kind=kLoop, calls=%fused_computation.75 | loop fusion | bytes 7077888 | tf_op jit(solution)/shard_map/slice | solution.py:33
  99.6 1.1 fusion
  100.7 1.1 fusion.4
  101.8 1.2 add_bitcast_fusion
  103.0 1.2 subtract_bitcast_fusion
  104.1 3.8 pad_maximum_fusion
  108.0 11.3 %copy.55 = f32[576,3,2,512]{3,2,1,0:T(2,128)} copy(f32[576,3,2,512]{3,0,1,2:T(8,128)} %pad_maximum_fusion) | data formatting | bytes 14155776 | tf_op jit(solution)/shard_map/stack | solution.py:37
  119.4 0.8 copy-done.4
  120.2 0.6 copy.57
  121.0 0.6 dynamic-slice
  122.3 47.9 %all_gather.12 = bf16[384,2,512]{2,0,1:T(8,128)(2,1)S(1)} all-gather(bf16[24,2,512]{2,0,1:T(8,128)(2,1)S(1)} %copy.46), channel_id=1, replica_groups=mesh['ga'=16,'pair'=16] {'pair'}, dimensions={0}, use_global_device_ids=true | all-gather | bytes 835584 | tf_op jit(solution)/shard_map/all_gather | solution.py:57
  170.7 0.5 fusion.14
  171.7 0.5 fusion.15
  172.1 0.7 pad_maximum_fusion.2
  172.8 170.3 %all-reduce.5.cloned.1.call-done = f32[576,3,2,512]{3,2,1,0:T(2,128)} async-done(((f32[576,3,2,512]{3,2,1,0:T(2,128)}), f32[576,3,2,512]{3,2,1,0:T(2,128)}) %all-reduce.5.cloned.1.call-update) | async-done | bytes 7077904
  343.1 1.6 constant_dynamic-slice_fusion
  344.7 64.8 %all-gather.8.cloned.1.call-done = bf16[256,3,2,512]{3,0,1,2:T(8,128)(2,1)} async-done(((bf16[16,3,2,512]{3,0,1,2:T(8,128)(2,1)}), bf16[256,3,2,512]{3,0,1,2:T(8,128)(2,1)}) %all-gather.8.cloned.1.call-update) | async-done | bytes 1572880 | tf_op jit(solution)/shard_map/all_gather | solution.py:72
  409.5 2.0 fusion.20
  411.6 1.9 fusion.21
  413.5 1.9 fusion.12
  415.5 0.8 fusion.13
  416.2 0.7 pad_maximum_fusion.1
  417.0 146.2 %all-reduce.7.cloned.1.call-done = (f32[384,3,2,24]{0,3,1,2:T(8,128)}, f32[256,3,2,36]{0,3,1,2:T(8,128)}) async-done(((f32[384,3,2,24]{0,3,1,2:T(8,128)}, f32[256,3,2,36]{0,3,1,2:T(8,128)}), (f32[384,3,2,24]{0,3,1,2:T(8,128)}, f32[256,3,2,36]{0,3,1,2:T(8,128)})) %all-reduce.7.cloned.1.call-update) | async-done | bytes 442384 | tf_op jit(solution)/shard_map/psum | solution.py:74
  563.2 1.1 copy.59
  564.2 2.7 stack.55
  566.9 18.8 %all-to-all-start = ((f32[16,256,3,2,36]{1,3,4,2,0:T(2,128)}), f32[16,256,3,2,36]{1,3,4,2,0:T(2,128)S(1)}, u32[]{:S(2)}, u32[]{:S(2)}) async-start(f32[16,256,3,2,36]{1,3,4,2,0:T(2,128)} %stack.55), calls=%async_computation | async-start | bytes 7077888 | tf_op jit(solution)/shard_map/all_to_all | solution.py:14
  585.8 0.5 all-gather.4.cloned.1.call-update
  586.3 0.6 fusion.32
  587.0 0.6 copy-done.7
  587.5 0.7 broadcast_add_fusion
  588.2 1.4 add.121
  589.7 0.6 pad_clamp_fusion.1
  590.3 0.7 fusion.31
  591.0 1.3 fusion.6
  592.3 93.6 %all-to-all-done = f32[16,256,3,2,36]{1,3,4,2,0:T(2,128)S(1)} async-done(((f32[16,256,3,2,36]{1,3,4,2,0:T(2,128)}), f32[16,256,3,2,36]{1,3,4,2,0:T(2,128)S(1)}, u32[]{:S(2)}, u32[]{:S(2)}) %all-to-all-start) | async-done | bytes 3538976 | tf_op jit(solution)/shard_map/all_to_all | solution.py:14
  685.9 3.0 copy.60
  688.8 8.3 %copy.61 = f32[256,3,2,576]{3,1,2,0:T(4,128)} copy(f32[256,3,2,576]{0,2,3,1:T(2,128)} %bitcast.103) | data formatting | bytes 7077888 | tf_op jit(solution)/shard_map/reshape | solution.py:13
  697.2 26.6 %gather_fusion.1 = f32[576,3,2,576]{3,1,2,0:T(4,128)} fusion(f32[256,3,2,576]{3,1,2,0:T(4,128)} %copy.61, s32[1024]{0:T(1024)S(1)} %pad_clamp_fusion), kind=kCustom, calls=%fused_computation.1 | custom fusion | bytes 15927552 | tf_op jit(solution)/shard_map/gather | solution.py:85
  723.8 7.3 multiply_reduce_fusion
  731.1 1.0 copy.63
  732.1 6.2 copy.47
  738.3 1.5 gather_fusion
  739.8 1.5 fusion.17
  741.3 0.7 copy.64
  (40 shorter events, 1.9 us)
Async XLA Ops:
  6.5 83.9 %all-gather.6.cloned.1.call-start = ((), (), s32[]{:S(2)}) async-start(), calls=%async_computation.2 | async-start | bytes 3760128 | tf_op jit(solution)/shard_map/all_gather | solution.py:67
  9.7 89.8 %copy-start = (bf16[3,2,512,512]{3,2,1,0:T(8,128)(2,1)S(1)}, bf16[3,2,512,512]{3,2,1,0:T(8,128)(2,1)}, u32[]{:S(2)}) copy-start(bf16[3,2,512,512]{3,2,1,0:T(8,128)(2,1)} %param.10) | copy-start | bytes 9437188
  9.7 333.4 %all-reduce.5.cloned.1.call-start = ((), (), s32[]{:S(2)}) async-start(), calls=%async_computation.4 | async-start | bytes 14155776
  119.3 0.9 copy-start.4
  119.3 1.6 copy-start.5
  119.3 1.7 copy-start.10
  119.3 2.9 copy-start.3
  119.3 2.9 copy-start.6
  119.3 290.2 %all-gather.8.cloned.1.call-start = ((), (), s32[]{:S(2)}) async-start(), calls=%async_computation.3 | async-start | bytes 1671168 | tf_op jit(solution)/shard_map/all_gather | solution.py:72
  120.9 442.3 %all-reduce.7.cloned.1.call-start = ((), (), s32[]{:S(2)}) async-start(), calls=%async_computation.5 | async-start | bytes 933888 | tf_op jit(solution)/shard_map/psum | solution.py:74
  409.5 5.9 copy-start.1
  566.9 19.4 %copy-start.9 = (s32[384]{0:T(512)S(1)}, s32[384]{0:T(512)}, u32[]{:S(2)}) copy-start(s32[384]{0:T(512)} %param.15) | copy-start | bytes 4612
  566.9 118.9 %all-to-all-start = ((f32[16,256,3,2,36]{1,3,4,2,0:T(2,128)}), f32[16,256,3,2,36]{1,3,4,2,0:T(2,128)S(1)}, u32[]{:S(2)}, u32[]{:S(2)}) async-start(f32[16,256,3,2,36]{1,3,4,2,0:T(2,128)} %stack.55), calls=%async_computation | async-start | bytes 7077888 | tf_op jit(solution)/shard_map/all_to_all | solution.py:14
  585.7 146.4 %all-gather.4.cloned.1.call-start = ((), (), s32[]{:S(2)}) async-start(), calls=%async_computation.1 | async-start | bytes 3760128 | tf_op jit(solution)/shard_map/all_gather | solution.py:77
  587.0 0.6 copy-start.7
  697.2 26.6 %copy-start.2 = (f32[576,576]{1,0:T(8,128)S(1)}, f32[576,576]{1,0:T(8,128)}, u32[]{:S(2)}) copy-start(f32[576,576]{1,0:T(8,128)} %fusion.6) | copy-start | bytes 3981316
  732.1 7.7 %copy-start.8 = (s32[24]{0:T(128)S(1)}, s32[24]{0:T(128)}, u32[]{:S(2)}) copy-start(s32[24]{0:T(128)} %copy-done.7) | copy-start | bytes 292
Sparse Core Ops, SparseCore 0:
  9.8 80.5 all-gather.5
  119.5 223.6 all-reduce.4
  345.9 63.5 all-gather.7
  417.1 146.0 all-reduce.6
  589.0 96.0 all-gather.3
